TPU v7x, 32 devices: a whole 2x2x4 slice. The times are simulated.
32 devices in a mesh: clip: 2 (over x), tile: 16 (over z, y, core).
Axes of the slice: x: 2, y: 2, z: 4, core: 2. Of those that a mesh axis runs over, the one named last changes fastest.
Arguments:
- latent: bfloat16 [8, 128, 32, 128], P('clip', 'tile'), parts along dimension 0, may hold values from -6 to 6
- cotangent: bfloat16 [8, 256, 64, 128], P('clip', 'tile'), parts along dimension 0, may hold values from -6 to 6
- kernel: bfloat16 [3, 3, 3, 128, 128], replicated, may hold values from -0.109375 to 0.109375
- ramp_lengths: int32 [32], P('clip'), parts along dimension 0, may hold values from 1 to 4
Outputs:
- latent_grad: bfloat16 [8, 128, 32, 128], P('clip', 'tile'), parts along dimension 0
- kernel_grad: float32 [256, 3456], P(('clip', 'tile')), parts along dimension 0
There are 2 independent parts, one for each index of `clip`. A program takes and returns all parts, laid end to end along the dimension named above; an argument that names none is the same for every part. Nothing has to cross between parts.
Inputs may be any that keep to these rules, and one draw needn't show every extreme that they name: `ramp_lengths`: entry t (t >= 1) is the ramp length of the boundary between tiles t - 1 and t; entry 0 is not used.
All inputs are finite; a program needn't handle non-finite values.
Results may differ from a plain program's by a relative error of at most 0.0031.
Values may be sent and summed in bfloat16 or wider, within the bound.
A program may use at most 128 MiB of HBM per device.

v0:
```python
import functools
import math

import jax
import jax.numpy as jnp
from jax import lax
from jax.experimental import pallas as pl
from jax.experimental.pallas import tpu as pltpu
from jax.sharding import PartitionSpec as P

OV = 1
MESH = pl.DeviceIdType.MESH
F32 = jnp.float32
BF16 = jnp.bfloat16
EDGE = 8


def rise(offset, length):
    shift_rows = lax.shift_right_arithmetic(4 * OV - length, jnp.ones_like(length))
    value = (offset - shift_rows + 1).astype(F32) / (length + 1).astype(F32)
    return jnp.clip(value, 0.0, 1.0)


def body(tiles, fused, norm, ramp_ref, lat_ref, cot_ref, k_ref, lg_ref, kg_ref, *scratch):
    if fused:
        (halo_lo, halo_hi, pad, lhs, gh, gl, kt_ref, halo_send, halo_recv,
         part, core_buf, send_buf, recv_buf, core_send, core_recv, far_send, far_recv) = scratch
    else:
        halo_lo, halo_hi, pad, lhs, gh, gl, kt_ref, halo_send, halo_recv = scratch
    frames, band, width, chans = lat_ref.shape
    wide = 2 * width
    area = band * width
    me = lax.axis_index("tile")
    core = lax.rem(me, 2)
    chip = lax.div(me, 2)
    chips = tiles // 2
    share = chans // tiles

    halo_lo[...] = jnp.zeros_like(halo_lo)
    halo_hi[...] = jnp.zeros_like(halo_hi)
    barrier = pltpu.get_barrier_semaphore()
    for d in range(1, tiles):
        pl.semaphore_signal(
            barrier, inc=1, device_id={"tile": lax.rem(me + d, tiles)}, device_id_type=MESH
        )

    for f in range(frames):
        turned = lat_ref[f].reshape(area, chans).T
        for kt in range(3):
            g_frame = f + 2 - kt
            if g_frame < frames:
                lhs[kt * chans : (kt + 1) * chans, g_frame * area : (g_frame + 1) * area] = turned
    for kt in range(2):
        for g_frame in range(2 - kt):
            lhs[kt * chans : (kt + 1) * chans, g_frame * area : (g_frame + 1) * area] = jnp.zeros(
                (chans, area), BF16
            )
    pad[:, :EDGE] = jnp.zeros((band, EDGE, chans), F32)
    pad[:, EDGE + wide :] = jnp.zeros((band, EDGE, chans), F32)
    upper = jnp.full((1, chans), ramp_ref[lax.min(me + 1, tiles - 1)], jnp.int32)
    lower = jnp.full((1, chans), ramp_ref[me], jnp.int32)
    has_upper = jnp.where(me <= tiles - 2, 1.0, 0.0).astype(F32)
    has_lower = jnp.where(me >= 1, 1.0, 0.0).astype(F32)
    upper_w = 1.0 - has_upper * rise(jnp.zeros_like(upper), upper)
    lower_w = 1.0 - has_lower * (1.0 - rise(jnp.full_like(lower, 3), lower))

    pl.semaphore_wait(barrier, tiles - 1)

    to_upper = pltpu.make_async_remote_copy(
        src_ref=cot_ref.at[:, 2 * band - 1], dst_ref=halo_lo, send_sem=halo_send.at[0],
        recv_sem=halo_recv.at[0], device_id={"tile": lax.rem(me + 1, tiles)}, device_id_type=MESH,
    )
    to_lower = pltpu.make_async_remote_copy(
        src_ref=cot_ref.at[:, 0], dst_ref=halo_hi, send_sem=halo_send.at[1],
        recv_sem=halo_recv.at[1], device_id={"tile": lax.rem(me + tiles - 1, tiles)}, device_id_type=MESH,
    )

    @pl.when(me < tiles - 1)
    def _():
        to_upper.start()

    @pl.when(me > 0)
    def _():
        to_lower.start()

    def build(kr):
        def one_frame(f, carry):
            for q in range(band):
                first, second = 2 * q + 1 - kr, 2 * q + 2 - kr
                low = (halo_lo[f] if first < 0 else cot_ref[f, first]).astype(F32)
                high = (halo_hi[f] if second == 2 * band else cot_ref[f, second]).astype(F32)
                if kr == 0 and q == band - 2:
                    high = high * upper_w
                if kr == 2 and q == 1:
                    low = low * lower_w
                pad[q, EDGE : EDGE + wide] = low + high
                left = pad[q, pl.ds(EDGE - 1, width, stride=2)]
                even = pad[q, pl.ds(EDGE, width, stride=2)]
                odd = pad[q, pl.ds(EDGE + 1, width, stride=2)]
                right = pad[q, pl.ds(EDGE + 2, width, stride=2)]
                rows = pl.ds(pl.multiple_of(f * area + q * width, width), width)
                for kc, box in enumerate((odd + right, even + odd, left + even)):
                    top = box.astype(BF16)
                    gh[kr, rows, kc * chans : (kc + 1) * chans] = top
                    gl[kr, rows, kc * chans : (kc + 1) * chans] = (box - top.astype(F32)).astype(BF16)
            return carry

        lax.fori_loop(0, frames, one_frame, 0)

    def core_copy(kr):
        return pltpu.make_async_remote_copy(
            src_ref=part.at[kr, 1 - core], dst_ref=core_buf.at[kr], send_sem=core_send.at[kr],
            recv_sem=core_recv.at[kr], device_id={"tile": me + 1 - 2 * core}, device_id_type=MESH,
        )

    def far_copy(kr, d):
        target = lax.rem(chip + d, chips)
        return pltpu.make_async_remote_copy(
            src_ref=send_buf.at[kr, target], dst_ref=recv_buf.at[kr, d - 1],
            send_sem=far_send.at[kr, d - 1], recv_sem=far_recv.at[kr, d - 1],
            device_id={"tile": 2 * target + core}, device_id_type=MESH,
        )

    def kernel_part(kr):
        total = jnp.dot(lhs[...], gh[kr], preferred_element_type=F32)
        total = total + jnp.dot(lhs[...], gl[kr], preferred_element_type=F32)
        for kt in range(3):
            if fused:
                for owner in range(tiles):
                    start = kt * chans + owner * share
                    part[kr, owner % 2, owner // 2, kt] = total[start : start + share]
            else:
                kg_ref[:, (kt * 3 + kr) * 3 * chans : (kt * 3 + kr + 1) * 3 * chans] = total[
                    kt * chans : (kt + 1) * chans
                ]
        if fused:
            core_copy(kr).start()

    def pass_on(kr):
        if fused:
            core_copy(kr).wait_recv()
            send_buf[kr] = (part[kr, core] + core_buf[kr]).astype(BF16)
            for d in range(1, chips):
                far_copy(kr, d).start()

    build(1)
    kernel_part(1)

    @pl.when(me > 0)
    def _():
        to_upper.wait_recv()

    @pl.when(me < tiles - 1)
    def _():
        to_lower.wait_recv()

    build(0)
    pass_on(1)
    kernel_part(0)
    build(2)
    pass_on(0)
    kernel_part(2)

    for kr in range(3):
        for kc in range(3):
            for kt in range(3):
                kt_ref[kr, kc * chans : (kc + 1) * chans, kt * chans : (kt + 1) * chans] = k_ref[kt, kr, kc].T
    pass_on(2)

    sums = [None] * frames
    for f in range(frames):
        first_kt = max(0, 2 - f)
        rows = slice(f * area, (f + 1) * area)
        spread = jnp.zeros((area, (3 - first_kt) * chans), F32)
        for kr in range(3):
            taps = kt_ref[kr, :, first_kt * chans :]
            spread = spread + jnp.dot(gh[kr, rows], taps, preferred_element_type=F32)
            spread = spread + jnp.dot(gl[kr, rows], taps, preferred_element_type=F32)
        for kt in range(first_kt, 3):
            term = spread[:, (kt - first_kt) * chans : (kt - first_kt + 1) * chans]
            target = f - 2 + kt
            sums[target] = term if sums[target] is None else sums[target] + term
    for f in range(frames):
        lg_ref[f] = sums[f].astype(BF16).reshape(band, width, chans)

    @pl.when(me < tiles - 1)
    def _():
        to_upper.wait_send()

    @pl.when(me > 0)
    def _():
        to_lower.wait_send()

    if fused:
        for kr in (1, 0, 2):
            for d in range(1, chips):
                far_copy(kr, d).wait_recv()
            for kt in range(3):
                total = part[kr, core, chip, kt] + core_buf[kr, chip, kt]
                for d in range(1, chips):
                    total = total + recv_buf[kr, d - 1, kt].astype(F32)
                start = (kt * 3 + kr) * 3 * chans
                kg_ref[:, start : start + 3 * chans] = total / F32(norm)
        for kr in range(3):
            core_copy(kr).wait_send()
            for d in range(1, chips):
                far_copy(kr, d).wait_send()


def shards(tiles, latent, cotangent, kernel, ramp_lengths):
    frames, band, width, chans = latent.shape
    share = chans // tiles
    norm = math.sqrt(4 * frames * band * tiles * width)
    fused = share % 8 == 0 and tiles % 2 == 0
    chips = tiles // 2
    cols = 27 * chans
    dma = pltpu.SemaphoreType.DMA
    scratch = [
        pltpu.VMEM((frames, 2 * width, chans), BF16),
        pltpu.VMEM((frames, 2 * width, chans), BF16),
        pltpu.VMEM((band, 2 * width + 2 * EDGE, chans), F32),
        pltpu.VMEM((3 * chans, frames * band * width), BF16),
        pltpu.VMEM((3, frames * band * width, 3 * chans), BF16),
        pltpu.VMEM((3, frames * band * width, 3 * chans), BF16),
        pltpu.VMEM((3, 3 * chans, 3 * chans), BF16),
        dma((2,)),
        dma((2,)),
    ]
    if fused:
        scratch += [
            pltpu.VMEM((3, 2, chips, 3, share, 3 * chans), F32),
            pltpu.VMEM((3, chips, 3, share, 3 * chans), F32),
            pltpu.VMEM((3, chips, 3, share, 3 * chans), BF16),
            pltpu.VMEM((3, chips - 1, 3, share, 3 * chans), BF16),
            dma((3,)),
            dma((3,)),
            dma((3, chips - 1)),
            dma((3, chips - 1)),
        ]
    vmem = pl.BlockSpec(memory_space=pltpu.VMEM)
    latent_grad, kernel_grad = pl.pallas_call(
        functools.partial(body, tiles, fused, norm),
        out_shape=(
            jax.ShapeDtypeStruct(latent.shape, BF16),
            jax.ShapeDtypeStruct((share if fused else chans, cols), F32),
        ),
        in_specs=[pl.BlockSpec(memory_space=pltpu.SMEM), vmem, vmem, vmem],
        out_specs=(vmem, vmem),
        scratch_shapes=scratch,
        compiler_params=pltpu.CompilerParams(
            collective_id=0, has_side_effects=True, vmem_limit_bytes=48 * 2**20
        ),
    )(ramp_lengths, latent, cotangent, kernel)
    if not fused:
        kernel_grad = lax.psum_scatter(kernel_grad, "tile", scatter_dimension=0, tiled=True) / F32(norm)
    return latent_grad, kernel_grad


def solution(mesh):
    in_specs = (P("clip", "tile", None, None), P("clip", "tile", None, None), P(), P("clip"))
    out_specs = (P("clip", "tile", None, None), P(("clip", "tile"), None))
    return jax.shard_map(
        functools.partial(shards, mesh.shape["tile"]),
        mesh=mesh, in_specs=in_specs, out_specs=out_specs, check_vma=False,
    )
```

profile of v0, /device:TPU:0, one launch (start us, length us, event | category | flops | bytes accessed | tf_op | source)
XLA Modules:
  0.0 26.7 jit_solution(16025789868800077629)
XLA Ops:
  0.6 0.0 copy-start
  0.6 1.2 %copy-done = bf16[4,16,64,128]{3,2,1,0:T(8,128)(2,1)S(1)} copy-done((bf16[4,16,64,128]{3,2,1,0:T(8,128)(2,1)S(1)}, bf16[4,16,64,128]{3,2,1,0:T(8,128)(2,1)}, u32[]{:S(2)}) %copy-start) | copy-done | bytes 1048600
  1.9 0.0 copy-start.1
  1.9 1.2 %copy-done.1 = bf16[3,3,3,128,128]{4,3,2,1,0:T(8,128)(2,1)S(1)} copy-done((bf16[3,3,3,128,128]{4,3,2,1,0:T(8,128)(2,1)S(1)}, bf16[3,3,3,128,128]{4,3,2,1,0:T(8,128)(2,1)}, u32[]{:S(2)}) %copy-start.1) | copy-done | bytes 884760
  3.0 0.0 copy-start.2
  3.0 0.9 %copy-done.2 = bf16[4,8,32,128]{3,2,1,0:T(8,128)(2,1)S(1)} copy-done((bf16[4,8,32,128]{3,2,1,0:T(8,128)(2,1)S(1)}, bf16[4,8,32,128]{3,2,1,0:T(8,128)(2,1)}, u32[]{:S(2)}) %copy-start.2) | copy-done | bytes 262168
  4.0 0.0 copy-start.3
  4.0 0.7 %copy-done.3 = s32[16]{0:T(128)S(1)} copy-done((s32[16]{0:T(128)S(1)}, s32[16]{0:T(128)}, u32[]{:S(2)}) %copy-start.3) | copy-done | bytes 88
  4.6 20.8 %shard_map.59 = (bf16[4,8,32,128]{3,2,1,0:T(8,128)(2,1)S(1)}, f32[8,3456]{1,0:T(8,128)S(1)}) custom-call(s32[16]{0:T(128)S(1)} %copy-done.3, bf16[4,8,32,128]{3,2,1,0:T(8,128)(2,1)S(1)} %copy-done.2, bf16[4,16,64,128]{3,2,1,0:T(8,128)(2,1)S(1)} %copy-done, bf16[3,3,3,128,128]{4,3,2,1,0:T(8,128)(2,1)S(1)} %copy-done.1), custom_call_target="tpu_custom_call" | custom-call | tf_op jit(solution)/shard_map/pallas_call | solution.py:241
  25.4 0.7 %copy.8 = bf16[4,8,32,128]{3,2,1,0:T(8,128)(2,1)} copy(bf16[4,8,32,128]{3,2,1,0:T(8,128)(2,1)S(1)} %get-tuple-element.4) | data formatting | bytes 524288
  26.1 0.6 %copy.9 = f32[8,3456]{1,0:T(8,128)} copy(f32[8,3456]{1,0:T(8,128)S(1)} %get-tuple-element.5) | data formatting | bytes 221184
Async XLA Ops:
  0.6 1.2 %copy-start = (bf16[4,16,64,128]{3,2,1,0:T(8,128)(2,1)S(1)}, bf16[4,16,64,128]{3,2,1,0:T(8,128)(2,1)}, u32[]{:S(2)}) copy-start(bf16[4,16,64,128]{3,2,1,0:T(8,128)(2,1)} %cot_ref.1) | copy-start | bytes 3145732
  1.9 1.2 %copy-start.1 = (bf16[3,3,3,128,128]{4,3,2,1,0:T(8,128)(2,1)S(1)}, bf16[3,3,3,128,128]{4,3,2,1,0:T(8,128)(2,1)}, u32[]{:S(2)}) copy-start(bf16[3,3,3,128,128]{4,3,2,1,0:T(8,128)(2,1)} %k_ref.1) | copy-start | bytes 2654212
  3.0 0.9 %copy-start.2 = (bf16[4,8,32,128]{3,2,1,0:T(8,128)(2,1)S(1)}, bf16[4,8,32,128]{3,2,1,0:T(8,128)(2,1)}, u32[]{:S(2)}) copy-start(bf16[4,8,32,128]{3,2,1,0:T(8,128)(2,1)} %lat_ref.1) | copy-start | bytes 786436
  4.0 0.7 %copy-start.3 = (s32[16]{0:T(128)S(1)}, s32[16]{0:T(128)}, u32[]{:S(2)}) copy-start(s32[16]{0:T(128)} %ramp_ref.1) | copy-start | bytes 196
where the time goes:
time: 27 us; the launch traced here: 26.7 us
  Pallas kernels  20.8 us (77%)
  local copies, waits for them, and re-layouts  5.34 us (20%)
  between operations  0.65 us (2%)
    pallas_call x1, Pallas kernels, shards(): pl.pallas_call(functools.partial(body, tiles, fused, norm), out_shape=(ja...  20.8 us
    unnamed x10, local copies, waits for them, and re-layouts  5.34 us

commit v1 on v0

--- a/solution.py
+++ b/solution.py
@@ -21,12 +21,11 @@
     return jnp.clip(value, 0.0, 1.0)
 
 
-def body(tiles, fused, norm, ramp_ref, lat_ref, cot_ref, k_ref, lg_ref, kg_ref, *scratch):
+def body(tiles, fused, norm, ramp_in, lat_in, cot_in, k_in, lg_ref, kg_ref, *scratch):
+    (ramp_ref, lat_ref, cot_ref, k_ref, in_sem, cot_sem, halo_lo, halo_hi, pad, lhs, gh, gl, kt_ref,
+     halo_send, halo_recv) = scratch[:15]
     if fused:
-        (halo_lo, halo_hi, pad, lhs, gh, gl, kt_ref, halo_send, halo_recv,
-         part, core_buf, send_buf, recv_buf, core_send, core_recv, far_send, far_recv) = scratch
-    else:
-        halo_lo, halo_hi, pad, lhs, gh, gl, kt_ref, halo_send, halo_recv = scratch
+        (part, core_buf, send_buf, recv_buf, core_send, core_recv, far_send, far_recv) = scratch[15:]
     frames, band, width, chans = lat_ref.shape
     wide = 2 * width
     area = band * width
@@ -36,6 +35,18 @@
     chips = tiles // 2
     share = chans // tiles
 
+    def cot_frame(f):
+        return pltpu.make_async_copy(cot_in.at[f], cot_ref.at[f], cot_sem.at[f])
+
+    ramp_copy = pltpu.make_async_copy(ramp_in, ramp_ref, in_sem.at[0])
+    lat_copy = pltpu.make_async_copy(lat_in, lat_ref, in_sem.at[1])
+    k_copy = pltpu.make_async_copy(k_in, k_ref, in_sem.at[2])
+    ramp_copy.start()
+    for f in range(frames):
+        cot_frame(f).start()
+    lat_copy.start()
+    k_copy.start()
+
     halo_lo[...] = jnp.zeros_like(halo_lo)
     halo_hi[...] = jnp.zeros_like(halo_hi)
     barrier = pltpu.get_barrier_semaphore()
@@ -44,68 +55,46 @@
             barrier, inc=1, device_id={"tile": lax.rem(me + d, tiles)}, device_id_type=MESH
         )
 
-    for f in range(frames):
-        turned = lat_ref[f].reshape(area, chans).T
-        for kt in range(3):
-            g_frame = f + 2 - kt
-            if g_frame < frames:
-                lhs[kt * chans : (kt + 1) * chans, g_frame * area : (g_frame + 1) * area] = turned
-    for kt in range(2):
-        for g_frame in range(2 - kt):
-            lhs[kt * chans : (kt + 1) * chans, g_frame * area : (g_frame + 1) * area] = jnp.zeros(
-                (chans, area), BF16
-            )
-    pad[:, :EDGE] = jnp.zeros((band, EDGE, chans), F32)
-    pad[:, EDGE + wide :] = jnp.zeros((band, EDGE, chans), F32)
-    upper = jnp.full((1, chans), ramp_ref[lax.min(me + 1, tiles - 1)], jnp.int32)
-    lower = jnp.full((1, chans), ramp_ref[me], jnp.int32)
-    has_upper = jnp.where(me <= tiles - 2, 1.0, 0.0).astype(F32)
-    has_lower = jnp.where(me >= 1, 1.0, 0.0).astype(F32)
-    upper_w = 1.0 - has_upper * rise(jnp.zeros_like(upper), upper)
-    lower_w = 1.0 - has_lower * (1.0 - rise(jnp.full_like(lower, 3), lower))
-
-    pl.semaphore_wait(barrier, tiles - 1)
-
-    to_upper = pltpu.make_async_remote_copy(
-        src_ref=cot_ref.at[:, 2 * band - 1], dst_ref=halo_lo, send_sem=halo_send.at[0],
-        recv_sem=halo_recv.at[0], device_id={"tile": lax.rem(me + 1, tiles)}, device_id_type=MESH,
-    )
-    to_lower = pltpu.make_async_remote_copy(
-        src_ref=cot_ref.at[:, 0], dst_ref=halo_hi, send_sem=halo_send.at[1],
-        recv_sem=halo_recv.at[1], device_id={"tile": lax.rem(me + tiles - 1, tiles)}, device_id_type=MESH,
-    )
-
-    @pl.when(me < tiles - 1)
-    def _():
-        to_upper.start()
-
-    @pl.when(me > 0)
-    def _():
-        to_lower.start()
-
-    def build(kr):
-        def one_frame(f, carry):
-            for q in range(band):
-                first, second = 2 * q + 1 - kr, 2 * q + 2 - kr
-                low = (halo_lo[f] if first < 0 else cot_ref[f, first]).astype(F32)
-                high = (halo_hi[f] if second == 2 * band else cot_ref[f, second]).astype(F32)
-                if kr == 0 and q == band - 2:
-                    high = high * upper_w
-                if kr == 2 and q == 1:
-                    low = low * lower_w
-                pad[q, EDGE : EDGE + wide] = low + high
-                left = pad[q, pl.ds(EDGE - 1, width, stride=2)]
-                even = pad[q, pl.ds(EDGE, width, stride=2)]
-                odd = pad[q, pl.ds(EDGE + 1, width, stride=2)]
-                right = pad[q, pl.ds(EDGE + 2, width, stride=2)]
+    pad[:, :EDGE] = jnp.zeros((band + 3, EDGE, chans), F32)
+    pad[:, EDGE + wide :] = jnp.zeros((band + 3, EDGE, chans), F32)
+    def box_row(f, slot, low, high, targets):
+        pad[slot, EDGE : EDGE + wide] = low + high
+        left = pad[slot, pl.ds(EDGE - 1, width, stride=2)]
+        even = pad[slot, pl.ds(EDGE, width, stride=2)]
+        odd = pad[slot, pl.ds(EDGE + 1, width, stride=2)]
+        right = pad[slot, pl.ds(EDGE + 2, width, stride=2)]
+        for kc, box in enumerate((odd + right, even + odd, left + even)):
+            cols = slice(kc * chans, (kc + 1) * chans)
+            top = box.astype(BF16)
+            rest = (box - top.astype(F32)).astype(BF16)
+            for kr, q in targets:
                 rows = pl.ds(pl.multiple_of(f * area + q * width, width), width)
-                for kc, box in enumerate((odd + right, even + odd, left + even)):
-                    top = box.astype(BF16)
-                    gh[kr, rows, kc * chans : (kc + 1) * chans] = top
-                    gl[kr, rows, kc * chans : (kc + 1) * chans] = (box - top.astype(F32)).astype(BF16)
-            return carry
-
-        lax.fori_loop(0, frames, one_frame, 0)
+                gh[kr, rows, cols] = top
+                gl[kr, rows, cols] = rest
+
+    def build_middle(f, carry):
+        cot_frame(f).wait()
+        for q in range(band):
+            box_row(f, q, cot_ref[f, 2 * q].astype(F32), cot_ref[f, 2 * q + 1].astype(F32), ((1, q),))
+        return carry
+
+    def build_sides(f, carry):
+        for j in range(band + 1):
+            low = (halo_lo[f] if j == 0 else cot_ref[f, 2 * j - 1]).astype(F32)
+            high = (halo_hi[f] if j == band else cot_ref[f, 2 * j]).astype(F32)
+            plain = []
+            if j < band:
+                if j == 1:
+                    box_row(f, band + 1, low * lower_w, high, ((2, j),))
+                else:
+                    plain.append((2, j))
+            if j > 0:
+                if j == band - 1:
+                    box_row(f, band + 2, low, high * upper_w, ((0, j - 1),))
+                else:
+                    plain.append((0, j - 1))
+            box_row(f, j, low, high, plain)
+        return carry
 
     def core_copy(kr):
         return pltpu.make_async_remote_copy(
@@ -136,15 +125,54 @@
         if fused:
             core_copy(kr).start()
 
-    def pass_on(kr):
+    def to_owners(kr):
         if fused:
             core_copy(kr).wait_recv()
             send_buf[kr] = (part[kr, core] + core_buf[kr]).astype(BF16)
             for d in range(1, chips):
                 far_copy(kr, d).start()
 
-    build(1)
+    lax.fori_loop(0, frames, build_middle, 0)
+    pl.semaphore_wait(barrier, tiles - 1)
+
+    to_upper = pltpu.make_async_remote_copy(
+        src_ref=cot_in.at[:, 2 * band - 1], dst_ref=halo_lo, send_sem=halo_send.at[0],
+        recv_sem=halo_recv.at[0], device_id={"tile": lax.rem(me + 1, tiles)}, device_id_type=MESH,
+    )
+    to_lower = pltpu.make_async_remote_copy(
+        src_ref=cot_in.at[:, 0], dst_ref=halo_hi, send_sem=halo_send.at[1],
+        recv_sem=halo_recv.at[1], device_id={"tile": lax.rem(me + tiles - 1, tiles)}, device_id_type=MESH,
+    )
+
+    @pl.when(me < tiles - 1)
+    def _():
+        to_upper.start()
+
+    @pl.when(me > 0)
+    def _():
+        to_lower.start()
+
+    lat_copy.wait()
+    for f in range(frames):
+        turned = lat_ref[f].reshape(area, chans).T
+        for kt in range(3):
+            g_frame = f + 2 - kt
+            if g_frame < frames:
+                lhs[kt * chans : (kt + 1) * chans, g_frame * area : (g_frame + 1) * area] = turned
+    for kt in range(2):
+        for g_frame in range(2 - kt):
+            lhs[kt * chans : (kt + 1) * chans, g_frame * area : (g_frame + 1) * area] = jnp.zeros(
+                (chans, area), BF16
+            )
     kernel_part(1)
+    ramp_copy.wait()
+    upper = jnp.full((1, chans), ramp_ref[lax.min(me + 1, tiles - 1)], jnp.int32)
+    lower = jnp.full((1, chans), ramp_ref[me], jnp.int32)
+    has_upper = jnp.where(me <= tiles - 2, 1.0, 0.0).astype(F32)
+    has_lower = jnp.where(me >= 1, 1.0, 0.0).astype(F32)
+    upper_w = 1.0 - has_upper * rise(jnp.zeros_like(upper), upper)
+    lower_w = 1.0 - has_lower * (1.0 - rise(jnp.full_like(lower, 3), lower))
+
 
     @pl.when(me > 0)
     def _():
@@ -154,18 +182,18 @@
     def _():
         to_lower.wait_recv()
 
-    build(0)
-    pass_on(1)
+    lax.fori_loop(0, frames, build_sides, 0)
+    to_owners(1)
     kernel_part(0)
-    build(2)
-    pass_on(0)
     kernel_part(2)
-
+    to_owners(0)
+
+    k_copy.wait()
     for kr in range(3):
         for kc in range(3):
             for kt in range(3):
                 kt_ref[kr, kc * chans : (kc + 1) * chans, kt * chans : (kt + 1) * chans] = k_ref[kt, kr, kc].T
-    pass_on(2)
+    to_owners(2)
 
     sums = [None] * frames
     for f in range(frames):
@@ -216,9 +244,15 @@
     cols = 27 * chans
     dma = pltpu.SemaphoreType.DMA
     scratch = [
+        pltpu.SMEM(ramp_lengths.shape, ramp_lengths.dtype),
+        pltpu.VMEM(latent.shape, BF16),
+        pltpu.VMEM(cotangent.shape, BF16),
+        pltpu.VMEM(kernel.shape, BF16),
+        dma((3,)),
+        dma((frames,)),
         pltpu.VMEM((frames, 2 * width, chans), BF16),
         pltpu.VMEM((frames, 2 * width, chans), BF16),
-        pltpu.VMEM((band, 2 * width + 2 * EDGE, chans), F32),
+        pltpu.VMEM((band + 3, 2 * width + 2 * EDGE, chans), F32),
         pltpu.VMEM((3 * chans, frames * band * width), BF16),
         pltpu.VMEM((3, frames * band * width, 3 * chans), BF16),
         pltpu.VMEM((3, frames * band * width, 3 * chans), BF16),
@@ -244,11 +278,11 @@
             jax.ShapeDtypeStruct(latent.shape, BF16),
             jax.ShapeDtypeStruct((share if fused else chans, cols), F32),
         ),
-        in_specs=[pl.BlockSpec(memory_space=pltpu.SMEM), vmem, vmem, vmem],
+        in_specs=[pl.BlockSpec(memory_space=pltpu.HBM)] * 4,
         out_specs=(vmem, vmem),
         scratch_shapes=scratch,
         compiler_params=pltpu.CompilerParams(
-            collective_id=0, has_side_effects=True, vmem_limit_bytes=48 * 2**20
+            collective_id=0, has_side_effects=True, vmem_limit_bytes=64 * 2**20
         ),
     )(ramp_lengths, latent, cotangent, kernel)
     if not fused:

time: 27 us -> 25 us (0.926)
  local copies, waits for them, and re-layouts: 5.34 us -> 2.36 us
  Pallas kernels: 20.8 us -> 21.9 us
    unnamed x10 -> x4, local copies, waits for them, and re-layouts: 5.34 us -> 2.36 us
    pallas_call x1, Pallas kernels: 20.8 us -> 21.9 us  [shards(): pl.pallas_call(functools.partial(body, tiles, fused, norm), out_shape=(ja...]
where the time goes in v1:
time: 25 us; the launch traced here: 24.9 us
  Pallas kernels  21.9 us (88%)
  local copies, waits for them, and re-layouts  2.36 us (9%)
  between operations  0.65 us (3%)
    pallas_call x1, Pallas kernels, shards(): pl.pallas_call(functools.partial(body, tiles, fused, norm), out_shape=(ja...  21.9 us
    unnamed x4, local copies, waits for them, and re-layouts  2.36 us

profile of v1, /device:TPU:0, one launch (start us, length us, event | category | flops | bytes accessed | tf_op | source)
XLA Modules:
  0.0 24.9 jit_solution(10241277715511999860)
XLA Ops:
  0.6 21.9 %shard_map.59 = (bf16[4,8,32,128]{3,2,1,0:T(8,128)(2,1)}, f32[8,3456]{1,0:T(8,128)}) custom-call(s32[16]{0:T(128)} %ramp_in.1, bf16[4,8,32,128]{3,2,1,0:T(8,128)(2,1)} %lat_in.1, bf16[4,16,64,128]{3,2,1,0:T(8,128)(2,1)} %cot_in.1, bf16[3,3,3,128,128]{4,3,2,1,0:T(8,128)(2,1)} %k_in.1), custom_call_target="tpu_custom_call" | custom-call | tf_op jit(solution)/shard_map/pallas_call | solution.py:275
  22.5 0.0 copy-start
  22.5 1.7 %copy.8 = bf16[4,8,32,128]{3,2,1,0:T(8,128)(2,1)} copy(bf16[4,8,32,128]{3,2,1,0:T(8,128)(2,1)} %get-tuple-element.4) | data formatting | bytes 524288
  24.2 0.0 copy-done
  24.2 0.6 %copy.9 = f32[8,3456]{1,0:T(8,128)} copy(f32[8,3456]{1,0:T(8,128)S(1)} %copy-done) | data formatting | bytes 221184
Async XLA Ops:
  22.5 1.7 %copy-start = (f32[8,3456]{1,0:T(8,128)S(1)}, f32[8,3456]{1,0:T(8,128)}, u32[]{:S(2)}) copy-start(f32[8,3456]{1,0:T(8,128)} %get-tuple-element.5) | copy-start | bytes 331780

commit v2 on v1

--- a/solution.py
+++ b/solution.py
@@ -132,7 +132,6 @@
             for d in range(1, chips):
                 far_copy(kr, d).start()
 
-    lax.fori_loop(0, frames, build_middle, 0)
     pl.semaphore_wait(barrier, tiles - 1)
 
     to_upper = pltpu.make_async_remote_copy(
@@ -152,6 +151,7 @@
     def _():
         to_lower.start()
 
+    lax.fori_loop(0, frames, build_middle, 0)
     lat_copy.wait()
     for f in range(frames):
         turned = lat_ref[f].reshape(area, chans).T

time: 25 us -> 24.6 us (0.984)
  Pallas kernels: 21.9 us -> 21.5 us
    pallas_call x1, Pallas kernels: 21.9 us -> 21.5 us  [shards(): pl.pallas_call(functools.partial(body, tiles, fused, norm), out_shape=(ja...]
where the time goes in v2:
time: 24.6 us; the launch traced here: 24.5 us
  Pallas kernels  21.5 us (87%)
  local copies, waits for them, and re-layouts  2.36 us (10%)
  between operations  0.65 us (3%)
    pallas_call x1, Pallas kernels, shards(): pl.pallas_call(functools.partial(body, tiles, fused, norm), out_shape=(ja...  21.5 us
    unnamed x4, local copies, waits for them, and re-layouts  2.36 us

profile of v2, /device:TPU:0, one launch (start us, length us, event | category | flops | bytes accessed | tf_op | source)
XLA Modules:
  0.0 24.5 jit_solution(10299055433762401267)
XLA Ops:
  0.6 21.5 %shard_map.59 = (bf16[4,8,32,128]{3,2,1,0:T(8,128)(2,1)}, f32[8,3456]{1,0:T(8,128)}) custom-call(s32[16]{0:T(128)} %ramp_in.1, bf16[4,8,32,128]{3,2,1,0:T(8,128)(2,1)} %lat_in.1, bf16[4,16,64,128]{3,2,1,0:T(8,128)(2,1)} %cot_in.1, bf16[3,3,3,128,128]{4,3,2,1,0:T(8,128)(2,1)} %k_in.1), custom_call_target="tpu_custom_call" | custom-call | tf_op jit(solution)/shard_map/pallas_call | solution.py:275
  22.1 0.0 copy-start
  22.1 1.7 %copy.8 = bf16[4,8,32,128]{3,2,1,0:T(8,128)(2,1)} copy(bf16[4,8,32,128]{3,2,1,0:T(8,128)(2,1)} %get-tuple-element.4) | data formatting | bytes 524288
  23.8 0.0 copy-done
  23.8 0.6 %copy.9 = f32[8,3456]{1,0:T(8,128)} copy(f32[8,3456]{1,0:T(8,128)S(1)} %copy-done) | data formatting | bytes 221184
Async XLA Ops:
  22.1 1.7 %copy-start = (f32[8,3456]{1,0:T(8,128)S(1)}, f32[8,3456]{1,0:T(8,128)}, u32[]{:S(2)}) copy-start(f32[8,3456]{1,0:T(8,128)} %get-tuple-element.5) | copy-start | bytes 331780

commit v3 on v2

--- a/solution.py
+++ b/solution.py
@@ -165,6 +165,12 @@
                 (chans, area), BF16
             )
     kernel_part(1)
+    k_copy.wait()
+    for kr in range(3):
+        for kc in range(3):
+            for kt in range(3):
+                kt_ref[kr, kc * chans : (kc + 1) * chans, kt * chans : (kt + 1) * chans] = k_ref[kt, kr, kc].T
+    to_owners(1)
     ramp_copy.wait()
     upper = jnp.full((1, chans), ramp_ref[lax.min(me + 1, tiles - 1)], jnp.int32)
     lower = jnp.full((1, chans), ramp_ref[me], jnp.int32)
@@ -183,17 +189,10 @@
         to_lower.wait_recv()
 
     lax.fori_loop(0, frames, build_sides, 0)
-    to_owners(1)
     kernel_part(0)
     kernel_part(2)
     to_owners(0)
 
-    k_copy.wait()
-    for kr in range(3):
-        for kc in range(3):
-            for kt in range(3):
-                kt_ref[kr, kc * chans : (kc + 1) * chans, kt * chans : (kt + 1) * chans] = k_ref[kt, kr, kc].T
-    to_owners(2)
 
     sums = [None] * frames
     for f in range(frames):
@@ -208,6 +207,8 @@
             term = spread[:, (kt - first_kt) * chans : (kt - first_kt + 1) * chans]
             target = f - 2 + kt
             sums[target] = term if sums[target] is None else sums[target] + term
+        if f == 0:
+            to_owners(2)
     for f in range(frames):
         lg_ref[f] = sums[f].astype(BF16).reshape(band, width, chans)
 

time: 24.6 us -> 24.1 us (0.980)
  Pallas kernels: 21.5 us -> 20.9 us
    pallas_call x1, Pallas kernels: 21.5 us -> 20.9 us  [shards(): pl.pallas_call(functools.partial(body, tiles, fused, norm), out_shape=(ja...]
where the time goes in v3:
time: 24.1 us; the launch traced here: 23.9 us
  Pallas kernels  20.9 us (87%)
  local copies, waits for them, and re-layouts  2.36 us (10%)
  between operations  0.65 us (3%)
    pallas_call x1, Pallas kernels, shards(): pl.pallas_call(functools.partial(body, tiles, fused, norm), out_shape=(ja...  20.9 us
    unnamed x4, local copies, waits for them, and re-layouts  2.36 us

profile of v3, /device:TPU:0, one launch (start us, length us, event | category | flops | bytes accessed | tf_op | source)
XLA Modules:
  0.0 23.9 jit_solution(2405540809117608443)
XLA Ops:
  0.6 20.9 %shard_map.59 = (bf16[4,8,32,128]{3,2,1,0:T(8,128)(2,1)}, f32[8,3456]{1,0:T(8,128)}) custom-call(s32[16]{0:T(128)} %ramp_in.1, bf16[4,8,32,128]{3,2,1,0:T(8,128)(2,1)} %lat_in.1, bf16[4,16,64,128]{3,2,1,0:T(8,128)(2,1)} %cot_in.1, bf16[3,3,3,128,128]{4,3,2,1,0:T(8,128)(2,1)} %k_in.1), custom_call_target="tpu_custom_call" | custom-call | tf_op jit(solution)/shard_map/pallas_call | solution.py:276
  21.6 0.0 copy-start
  21.6 1.7 %copy.8 = bf16[4,8,32,128]{3,2,1,0:T(8,128)(2,1)} copy(bf16[4,8,32,128]{3,2,1,0:T(8,128)(2,1)} %get-tuple-element.4) | data formatting | bytes 524288
  23.3 0.0 copy-done
  23.3 0.6 %copy.9 = f32[8,3456]{1,0:T(8,128)} copy(f32[8,3456]{1,0:T(8,128)S(1)} %copy-done) | data formatting | bytes 221184
Async XLA Ops:
  21.6 1.7 %copy-start = (f32[8,3456]{1,0:T(8,128)S(1)}, f32[8,3456]{1,0:T(8,128)}, u32[]{:S(2)}) copy-start(f32[8,3456]{1,0:T(8,128)} %get-tuple-element.5) | copy-start | bytes 331780
